TPU v7x, 32 devices: a whole 2x2x4 slice. The times are simulated.
32 devices in a mesh: groups: 2 (over y), slab: 4 (over z), sub: 4 (over x, core).
Axes of the slice: x: 2, y: 2, z: 4, core: 2. Of those that a mesh axis runs over, the one named last changes fastest.
Arguments:
- image: bfloat16 [2, 32, 128, 128], P(None, ('groups', 'slab', 'sub')), parts along dimension 1, may hold values from -6 to 6
- w_in: bfloat16 [9, 32, 2], replicated, may hold values from -2 to 2
- w_down2: bfloat16 [9, 64, 32], replicated, may hold values from -0.5 to 0.5
- w_down3: bfloat16 [9, 128, 64], replicated, may hold values from -0.375 to 0.375
- w_up3: bfloat16 [9, 64, 128], replicated, may hold values from -0.25 to 0.25
- w_up2: bfloat16 [9, 32, 64], replicated, may hold values from -0.375 to 0.375
- w_up1: bfloat16 [9, 32, 32], replicated, may hold values from -0.5 to 0.5
- w_out: bfloat16 [3, 32], replicated, may hold values from -1 to 1
Outputs:
- flows: float32 [4, 32, 128, 128], P(None, ('groups', 'slab', 'sub')), parts along dimension 1
There are 2 independent parts, one for each index of `groups`. A program takes and returns all parts, laid end to end along the dimension named above; an argument that names none is the same for every part. Nothing has to cross between parts.
All inputs are finite; a program needn't handle non-finite values.
Results may differ from a plain program's by a relative error of at most 0.024.
Values may be sent and summed in bfloat16 or wider, within the bound.
A program may use at most 128 MiB of HBM per device.

v0:
```python
import functools

import jax
import jax.numpy as jnp
from jax import lax
from jax.experimental import pallas as pl
from jax.experimental.pallas import tpu as pltpu
from jax.sharding import PartitionSpec as P

F32, BF16 = jnp.float32, jnp.bfloat16
BLOCKS = 16
LANES = 256
AXES = ("slab", "sub")

BANDS = {
    "down2": (32, 64, (0, 0, 1, 1, 2, 2, 3, 3, 4, 4, -1, -1), 0.25),
    "down3": (64, 128, (0, 0, 1, 1, 2, 2, -1, -1), 0.25),
    "up3": (128, 128, (0, 1, 2, -1), 1.0),
    "up2": (64, 64, (0, 1, 2, 3, 4, -1), 1.0),
    "up1": (32, 32, (0, 1, 2, 3, 4, 5, 6, 7, 8, None, None, -1), 1.0),
}


def tile_weights(weight, chan_in):
    flipped = jnp.swapaxes(weight, 1, 2)
    return jnp.tile(flipped, (1, 1, LANES // weight.shape[1]))


def build_band(name, tiled_ref, band_ref):
    chan, cell_lanes, cells, scale = BANDS[name]
    cell_of_lane = lax.broadcasted_iota(jnp.int32, (chan, LANES), 1) // cell_lanes
    depth = chan * len(cells)
    for down in range(3):
        taps = [tiled_ref[3 * down + c].astype(F32) * scale for c in range(3)]
        for number, cell in enumerate(cells):
            total = jnp.zeros((chan, LANES), F32)
            if cell is not None:
                for c in range(3):
                    total = jnp.where(cell_of_lane == cell - c + 1, taps[c], total)
            start = down * depth + number * chan
            band_ref[start : start + chan, :] = total.astype(BF16)


def build_in(tiled_ref, band_ref):
    shape = (128, LANES)
    row = lax.broadcasted_iota(jnp.int32, shape, 0)
    cell = lax.broadcasted_iota(jnp.int32, shape, 1) // 32
    tiled = tiled_ref[...].astype(F32)
    for down in range(3):
        total = jnp.zeros(shape, F32)
        for chan in range(2):
            for c in range(3):
                index = (3 * down + c) * 2 + chan
                total = jnp.where(row - 16 * chan - cell == c, tiled[index : index + 1, :], total)
        band_ref[128 * down : 128 * down + 128, :] = total.astype(BF16)


def build_out(tiled_ref, band_ref):
    shape = (LANES, 128)
    keep = lax.broadcasted_iota(jnp.int32, shape, 0) // 32 == lax.broadcasted_iota(
        jnp.int32, shape, 1
    ) % 8
    for out in range(3):
        value = tiled_ref[:, out : out + 1].astype(F32)
        band_ref[:, 128 * out : 128 * out + 128] = jnp.where(keep, value, 0.0).astype(BF16)


def neighbours(values):
    count = values.shape[0]
    block = lax.broadcasted_iota(jnp.int32, (count, BLOCKS, 128), 1)
    right = pltpu.roll(values[..., :128], 1, 1)
    left = pltpu.roll(values[..., 128:], BLOCKS - 1, 1)
    right = jnp.where(block == 0, 0.0, right)
    left = jnp.where(block == BLOCKS - 1, 0.0, left)
    return right, left


def narrow_halo(values):
    right, left = neighbours(values)
    lane = lax.broadcasted_iota(jnp.int32, right.shape, 2)
    return jnp.where(lane < 64, right, left)


def store_narrow(ref, start, values):
    count = values.shape[0]
    ref[pl.ds(start, count), :, :256] = values.astype(BF16)
    ref[pl.ds(start, count), :, 256:] = narrow_halo(values).astype(BF16)


def store_wide(ref, start, values):
    count = values.shape[0]
    right, left = neighbours(values)
    ref[pl.ds(start, count), :, :256] = values.astype(BF16)
    ref[pl.ds(start, count), :, 256:384] = right.astype(BF16)
    ref[pl.ds(start, count), :, 384:] = left.astype(BF16)


def conv(ref, band_ref, start, count, span):
    depth = ref.shape[2]
    parts = [ref[pl.ds(start + down * span, count)] for down in range(3)]
    rows = jnp.concatenate(parts, axis=-1).reshape(count * BLOCKS, 3 * depth)
    total = jnp.dot(rows, band_ref[...], preferred_element_type=F32)
    return jnp.maximum(total, 0.0).reshape(count, BLOCKS, LANES)


def pair_sum(values, span):
    count = values.shape[0]
    pairs = values.reshape(count // (2 * span), 2, span, BLOCKS, LANES)
    return (pairs[:, 0] + pairs[:, 1]).reshape(count // 2, BLOCKS, LANES)


def twice(values, span):
    count = values.shape[0]
    rows = values.reshape(count // span, 1, span, BLOCKS, LANES)
    return jnp.broadcast_to(rows, (count // span, 2, span, BLOCKS, LANES)).reshape(
        2 * count, BLOCKS, LANES
    )


def clear_edges(ref, height, span):
    zero = jnp.zeros((span,) + tuple(ref.shape[1:]), ref.dtype)
    ref[pl.ds(0, span)] = zero
    ref[pl.ds((height + 1) * span, span)] = zero


def chunks(total, count, body):
    steps = total // count
    if steps == 1:
        body(0)
    else:

        def step(i, carry):
            body(i * count)
            return carry

        lax.fori_loop(0, steps, step, 0)


def unet(height, span, load, emit, bands, scratch):
    b_in, b_down2, b_down3, b_up3, b_up2, b_up1, b_out = bands
    win, a1, p1, a2, p2, a3, s2, s1 = scratch
    for ref, rows in ((win, height), (p1, height // 2), (p2, height // 4), (a3, height // 4)):
        clear_edges(ref, rows, span)
    clear_edges(s2, height // 2, span)
    clear_edges(s1, height, span)
    units = height * span
    count = max(32, 2 * span)

    def fill(g):
        shape = (count, BLOCKS, 128)
        lane = lax.broadcasted_iota(jnp.int32, shape, 2)
        block = lax.broadcasted_iota(jnp.int32, shape, 1)
        outside = ((block == BLOCKS - 1) & (lane % 16 == 0)) | ((block == 0) & (lane % 16 == 9))
        rolled = []
        for chan in range(2):
            row = pltpu.roll(load(chan, g, count).astype(F32), 9 + 16 * chan, 1)
            row = jnp.broadcast_to(row[:, None, :], shape)
            rolled.append(pltpu.roll(row, 0, 2, stride=8, stride_axis=1))
        merged = jnp.where(lane < 16, rolled[0], rolled[1])
        win[pl.ds(g + span, count)] = jnp.where(outside, 0.0, merged).astype(BF16)

    chunks(units, count, fill)

    def level1(g):
        values = conv(win, b_in, g, count, span)
        a1[pl.ds(g, count)] = values.astype(BF16)
        store_narrow(p1, g // 2 + span, pair_sum(values, span))

    chunks(units, count, level1)

    def level2(g):
        values = conv(p1, b_down2, g, count, span)
        a2[pl.ds(g, count)] = values.astype(BF16)
        store_wide(p2, g // 2 + span, pair_sum(values, span))

    chunks(units // 2, count, level2)

    def level3(g):
        store_wide(a3, g + span, conv(p2, b_down3, g, count, span))

    chunks(units // 4, count, level3)

    def level3_up(g):
        values = twice(conv(a3, b_up3, g, count, span), span)
        skip = a2[pl.ds(2 * g, 2 * count)].astype(F32)
        store_narrow(s2, 2 * g + span, values + skip)

    chunks(units // 4, count, level3_up)

    def level2_up(g):
        values = twice(conv(s2, b_up2, g, count, span), span)
        skip = a1[pl.ds(2 * g, 2 * count)].astype(F32)
        store_narrow(s1, 2 * g + span, values + skip)

    chunks(units // 2, count, level2_up)

    def level1_up(g):
        values = conv(s1, b_up1, g, count, span).astype(BF16)
        spread = jnp.dot(
            values.reshape(count * BLOCKS, LANES), b_out[...], preferred_element_type=F32
        ).reshape(count, BLOCKS, 384)
        shape = (count, BLOCKS, 384)
        lane = lax.broadcasted_iota(jnp.int32, shape, 2)
        block = lax.broadcasted_iota(jnp.int32, shape, 1)
        emit(g, jnp.sum(jnp.where(lane % 128 // 8 == BLOCKS - 1 - block, spread, 0.0), axis=1))

    chunks(units, count, level1_up)


def unit_scratch(height, span):
    def spec(rows, lanes, edge=True):
        return pltpu.VMEM(((rows + (2 if edge else 0)) * span, BLOCKS, lanes), BF16)

    return [
        spec(height, 128),
        spec(height, 256, False),
        spec(height // 2, 384),
        spec(height // 2, 256, False),
        spec(height // 4, 512),
        spec(height // 4, 512),
        spec(height // 2, 384),
        spec(height, 384),
    ]


BAND_SCRATCH = [
    pltpu.VMEM((384, 256), BF16),
    pltpu.VMEM((1152, 256), BF16),
    pltpu.VMEM((1536, 256), BF16),
    pltpu.VMEM((1536, 256), BF16),
    pltpu.VMEM((1152, 256), BF16),
    pltpu.VMEM((1152, 256), BF16),
    pltpu.VMEM((256, 384), BF16),
]


def build_all(tiled, bands):
    build_in(tiled[0], bands[0])
    for name, source, band in zip(("down2", "down3", "up3", "up2", "up1"), tiled[1:6], bands[1:6]):
        build_band(name, source, band)
    build_out(tiled[6], bands[6])


def net_kernel(height, span, x_ref, *refs):
    tiled, out_ref, bands, scratch = refs[:7], refs[7], refs[8:15], refs[15:]
    build_all(tiled, bands)

    def load(chan, start, count):
        return x_ref[chan, pl.ds(pl.multiple_of(start, 16), count), :]

    def emit(start, values):
        count = values.shape[0]
        out_ref[pl.ds(pl.multiple_of(start, 16), count), :] = values.astype(out_ref.dtype)

    unet(height, span, load, emit, bands, scratch)


def run_net(x, tiled, height, span, dtype):
    return pl.pallas_call(
        functools.partial(net_kernel, height, span),
        out_shape=jax.ShapeDtypeStruct((height * span, 384), dtype),
        in_specs=[pl.BlockSpec(memory_space=pltpu.VMEM)] * 8,
        out_specs=pl.BlockSpec(memory_space=pltpu.VMEM),
        scratch_shapes=BAND_SCRATCH + unit_scratch(height, span),
        compiler_params=pltpu.CompilerParams(vmem_limit_bytes=48 << 20),
    )(x, *tiled)


def prepare(weights):
    w_in, w_out = weights[0], weights[6]
    tiled_in = jnp.tile(jnp.swapaxes(w_in, 1, 2).reshape(18, 32), (1, 8))
    tiled_out = jnp.tile(jnp.swapaxes(w_out, 0, 1), (8, 1))
    return [tiled_in] + [tile_weights(w, w.shape[2]) for w in weights[1:6]] + [tiled_out]


def shards(image, *weights):
    tiled = prepare(weights)
    chan, _, extent, _ = image.shape
    plane = image[:, 0]
    peers = lax.axis_size(AXES)
    cut = extent // peers
    both = jnp.stack([plane, jnp.swapaxes(plane, 1, 2)])
    send = jnp.transpose(both.reshape(2, chan, peers, cut, extent), (2, 1, 0, 3, 4))
    got = lax.all_to_all(send, AXES, split_axis=0, concat_axis=0, tiled=True)
    cross = jnp.transpose(got, (1, 0, 2, 3, 4)).reshape(chan, peers * 2 * cut, extent)
    flat = run_net(plane, tiled, extent, 1, F32).reshape(extent, 3, extent)
    result = run_net(cross, tiled, peers, 2 * cut, BF16).reshape(peers, 2, cut, 3, extent)
    back = lax.all_to_all(result, AXES, split_axis=0, concat_axis=0, tiled=True)
    back = jnp.transpose(back, (1, 3, 0, 2, 4)).reshape(2, 3, extent, extent).astype(F32)
    xz = back[0]
    yz = jnp.swapaxes(back[1], 1, 2)
    flow_z = (xz[0] + yz[0]) * 0.5
    flow_y = (flat[:, 0] + yz[1]) * 0.5
    flow_x = (flat[:, 1] + xz[1]) * 0.5
    prob = (flat[:, 2] + xz[2] + yz[2]) / 3.0
    return jnp.stack([flow_z, flow_y, flow_x, prob])[:, None]


def solution(mesh):
    split = P(None, ("groups", "slab", "sub"), None, None)
    return jax.shard_map(
        shards,
        mesh=mesh,
        in_specs=(split,) + (P(),) * 7,
        out_specs=split,
        check_vma=False,
    )
```

profile of v0, /device:TPU:0, one launch (start us, length us, event | category | flops | bytes accessed | tf_op | source)
XLA Modules:
  0.0 53.3 jit_solution(5837120881113263818)
XLA Ops:
  0.0 1.0 %copy.47 = bf16[2,128,128]{2,1,0:T(8,128)(2,1)S(1)} copy(bf16[2,128,128]{1,2,0:T(8,128)(2,1)} %bitcast.59) | data formatting | bytes 131072 | tf_op jit(solution)/shard_map/transpose | solution.py:282
  1.1 0.7 %copy.48 = bf16[16,2,2,8,128]{4,3,1,2,0:T(8,128)(2,1)} copy(bf16[16,2,2,8,128]{4,3,0,1,2:T(8,128)(2,1)S(1)} %maximum_bitcast_fusion.1) | data formatting | bytes 262144 | tf_op jit(solution)/shard_map/transpose | solution.py:283
  1.7 7.5 %all-to-all-start = ((bf16[16,2,2,8,128]{4,3,1,2,0:T(8,128)(2,1)}), bf16[16,2,2,8,128]{4,3,1,2,0:T(8,128)(2,1)S(1)}, u32[]{:S(2)}, u32[]{:S(2)}) async-start(bf16[16,2,2,8,128]{4,3,1,2,0:T(8,128)(2,1)} %copy.48), calls=%async_computation | async-start | bytes 262144 | tf_op jit(solution)/shard_map/all_to_all | solution.py:284
  9.3 0.1 tile.71
  9.4 0.2 copy.52.refs_3_
  9.6 0.6 %copy-done.4 = bf16[9,32,64]{2,1,0:T(8,128)(2,1)S(1)} copy-done((bf16[9,32,64]{2,1,0:T(8,128)(2,1)S(1)}, bf16[9,32,64]{2,1,0:T(8,128)(2,1)}, u32[]{:S(2)}) %copy-start.4) | copy-done | bytes 36888
  10.3 0.1 tile.73
  10.4 0.2 copy.53.refs_4_
  10.6 0.6 %copy-done.3 = bf16[9,32,32]{2,1,0:T(8,128)(2,1)S(1)} copy-done((bf16[9,32,32]{2,1,0:T(8,128)(2,1)S(1)}, bf16[9,32,32]{2,1,0:T(8,128)(2,1)}, u32[]{:S(2)}) %copy-start.3) | copy-done | bytes 18456
  11.3 0.1 copy.50
  11.4 0.1 tile.75
  11.5 0.4 tile.76.refs_5_
  11.9 0.5 copy-done.1
  12.4 0.2 tile.69
  12.6 0.2 tile.70.refs_2_
  12.8 0.7 %copy-done.5 = bf16[9,64,32]{1,2,0:T(8,128)(2,1)S(1)} copy-done((bf16[9,64,32]{1,2,0:T(8,128)(2,1)S(1)}, bf16[9,64,32]{1,2,0:T(8,128)(2,1)}, u32[]{:S(2)}) %copy-start.5) | copy-done | bytes 36888
  13.4 0.1 tile.33
  13.5 0.2 tile.68.refs_1_
  13.8 0.7 %copy-done.7 = bf16[3,32]{1,0:T(4,128)(2,1)S(1)} copy-done((bf16[3,32]{1,0:T(4,128)(2,1)S(1)}, bf16[3,32]{1,0:T(4,128)(2,1)}, u32[]{:S(2)}) %copy-start.7) | copy-done | bytes 216
  14.4 0.1 copy.51
  14.5 0.6 %copy-done.6 = bf16[9,32,2]{1,2,0:T(2,128)(2,1)S(1)} copy-done((bf16[9,32,2]{1,2,0:T(2,128)(2,1)S(1)}, bf16[9,32,2]{1,2,0:T(2,128)(2,1)}, u32[]{:S(2)}) %copy-start.6) | copy-done | bytes 1176
  15.2 0.1 tile.32.refs_0_
  15.3 1.9 %all-to-all-done = bf16[16,2,2,8,128]{4,3,1,2,0:T(8,128)(2,1)S(1)} async-done(((bf16[16,2,2,8,128]{4,3,1,2,0:T(8,128)(2,1)}), bf16[16,2,2,8,128]{4,3,1,2,0:T(8,128)(2,1)S(1)}, u32[]{:S(2)}, u32[]{:S(2)}) %all-to-all-start) | async-done | bytes 131104 | tf_op jit(solution)/shard_map/all_to_all | solution.py:284
  17.2 20.0 %shard_map.82 = bf16[256,384]{1,0:T(8,128)(2,1)} custom-call(bf16[2,256,128]{2,1,0:T(8,128)(2,1)S(1)} %bitcast.62, bf16[18,256]{1,0:T(8,128)(2,1)S(1)} %tile.32.refs_0_, bf16[9,32,256]{2,1,0:T(8,128)(2,1)S(1)} %tile.68.refs_1_, bf16[9,64,256]{2,1,0:T(8,128)(2,1)S(1)} %tile.70.refs_2_, bf16[9,128,256]{2,1,0:T(8,128)(2,1)S(1)} %copy.52.refs_3_, ...), custom_call_target="tpu_custom_call" | custom-call | tf_op jit(solution)/shard_map/pallas_call | solution.py:259
  37.2 4.1 %all-to-all-start.1 = ((bf16[16,2,8,3,128]{4,2,3,1,0:T(8,128)(2,1)}), bf16[16,2,8,3,128]{4,2,3,1,0:T(8,128)(2,1)S(1)}, u32[]{:S(2)}, u32[]{:S(2)}) async-start(bf16[16,2,8,3,128]{4,2,3,1,0:T(8,128)(2,1)} %bitcast.17), calls=%async_computation.1 | async-start | bytes 393216 | tf_op jit(solution)/shard_map/all_to_all | solution.py:288
  41.4 10.5 %shard_map.83 = f32[128,384]{1,0:T(8,128)S(1)} custom-call(bf16[2,128,128]{2,1,0:T(8,128)(2,1)S(1)} %bitcast.61, bf16[18,256]{1,0:T(8,128)(2,1)S(1)} %tile.32.refs_0_, bf16[9,32,256]{2,1,0:T(8,128)(2,1)S(1)} %tile.68.refs_1_, bf16[9,64,256]{2,1,0:T(8,128)(2,1)S(1)} %tile.70.refs_2_, bf16[9,128,256]{2,1,0:T(8,128)(2,1)S(1)} %copy.52.refs_3_, ...), custom_call_target="tpu_custom_call" | custom-call | tf_op jit(solution)/shard_map/pallas_call | solution.py:259
  51.9 0.1 copy.58
  52.0 0.1 copy.63
  52.1 0.1 copy.64
  52.2 0.1 copy.65
  52.4 0.1 copy.55
  52.6 0.7 %maximum_bitcast_fusion = f32[4,1,128,128]{3,2,1,0:T(8,128)} fusion(f32[1,128,128]{2,1,0:T(8,128)S(1)} %get-tuple-element.6, f32[1,128,128]{2,1,0:T(8,128)S(1)} %get-tuple-element.7, f32[1,128,128]{2,1,0:T(8,128)S(1)} %get-tuple-element.8, f32[1,128,128]{2,1,0:T(8,128)S(1)} %get-tuple-element.5), kind=kLoop, calls=%fused_computation.2 | loop fusion | flops 196608 | bytes 524288 | tf_op jit(solution)/shard_map/broadcast_in_dim | solution.py:296
  (20 shorter events, 0.2 us)
Async XLA Ops:
  0.0 1.0 %copy-start = (bf16[2,1,128,128]{3,2,1,0:T(8,128)(2,1)S(1)}, bf16[2,1,128,128]{3,2,1,0:T(8,128)(2,1)}, u32[]{:S(2)}) copy-start(bf16[2,1,128,128]{3,2,1,0:T(8,128)(2,1)} %param.8) | copy-start | bytes 196612
  1.7 7.5 %copy-start.2 = (bf16[9,64,128]{2,1,0:T(8,128)(2,1)S(1)}, bf16[9,64,128]{2,1,0:T(8,128)(2,1)}, u32[]{:S(2)}) copy-start(bf16[9,64,128]{2,1,0:T(8,128)(2,1)} %param.12) | copy-start | bytes 442372
  1.7 15.4 %all-to-all-start = ((bf16[16,2,2,8,128]{4,3,1,2,0:T(8,128)(2,1)}), bf16[16,2,2,8,128]{4,3,1,2,0:T(8,128)(2,1)S(1)}, u32[]{:S(2)}, u32[]{:S(2)}) async-start(bf16[16,2,2,8,128]{4,3,1,2,0:T(8,128)(2,1)} %copy.48), calls=%async_computation | async-start | bytes 262144 | tf_op jit(solution)/shard_map/all_to_all | solution.py:284
  9.4 0.9 %copy-start.4 = (bf16[9,32,64]{2,1,0:T(8,128)(2,1)S(1)}, bf16[9,32,64]{2,1,0:T(8,128)(2,1)}, u32[]{:S(2)}) copy-start(bf16[9,32,64]{2,1,0:T(8,128)(2,1)} %param.13) | copy-start | bytes 110596
  10.4 0.9 %copy-start.3 = (bf16[9,32,32]{2,1,0:T(8,128)(2,1)S(1)}, bf16[9,32,32]{2,1,0:T(8,128)(2,1)}, u32[]{:S(2)}) copy-start(bf16[9,32,32]{2,1,0:T(8,128)(2,1)} %param.14) | copy-start | bytes 55300
  11.5 0.9 %copy-start.1 = (bf16[9,128,64]{1,2,0:T(8,128)(2,1)S(1)}, bf16[9,128,64]{1,2,0:T(8,128)(2,1)}, u32[]{:S(2)}) copy-start(bf16[9,128,64]{1,2,0:T(8,128)(2,1)} %param.11) | copy-start | bytes 442372
  12.6 0.9 %copy-start.5 = (bf16[9,64,32]{1,2,0:T(8,128)(2,1)S(1)}, bf16[9,64,32]{1,2,0:T(8,128)(2,1)}, u32[]{:S(2)}) copy-start(bf16[9,64,32]{1,2,0:T(8,128)(2,1)} %param.10) | copy-start | bytes 110596
  13.8 0.7 %copy-start.7 = (bf16[3,32]{1,0:T(4,128)(2,1)S(1)}, bf16[3,32]{1,0:T(4,128)(2,1)}, u32[]{:S(2)}) copy-start(bf16[3,32]{1,0:T(4,128)(2,1)} %param.15) | copy-start | bytes 580
  14.4 0.7 %copy-start.6 = (bf16[9,32,2]{1,2,0:T(2,128)(2,1)S(1)}, bf16[9,32,2]{1,2,0:T(2,128)(2,1)}, u32[]{:S(2)}) copy-start(bf16[9,32,2]{1,2,0:T(2,128)(2,1)} %param.9) | copy-start | bytes 3460
  37.2 15.1 %all-to-all-start.1 = ((bf16[16,2,8,3,128]{4,2,3,1,0:T(8,128)(2,1)}), bf16[16,2,8,3,128]{4,2,3,1,0:T(8,128)(2,1)S(1)}, u32[]{:S(2)}, u32[]{:S(2)}) async-start(bf16[16,2,8,3,128]{4,2,3,1,0:T(8,128)(2,1)} %bitcast.17), calls=%async_computation.1 | async-start | bytes 393216 | tf_op jit(solution)/shard_map/all_to_all | solution.py:288
where the time goes:
time: 53.8 us; the launch traced here: 53.3 us
  Pallas kernels  30.5 us (57%)
  starting transfers between devices  11.6 us (22%)
  local copies, waits for them, and re-layouts  8.19 us (15%)
  waiting for transfers between devices  1.92 us (4%)
  other arithmetic  0.83 us (2%)
    pallas_call x2, Pallas kernels, run_net(): pl.pallas_call(functools.partial(net_kernel, height, span), out_shape=jax...  30.5 us
    all_to_all x1, starting transfers between devices, shards(): got = lax.all_to_all(send, AXES, split_axis=0, concat_axis=0, tiled=True)  7.49 us
    all_to_all x1, starting transfers between devices, shards(): back = lax.all_to_all(result, AXES, split_axis=0, concat_axis=0, tiled=True)  4.11 us
    unnamed x19, local copies, waits for them, and re-layouts  4.01 us
    all_to_all x1, waiting for transfers between devices, shards(): got = lax.all_to_all(send, AXES, split_axis=0, concat_axis=0, tiled=True)  1.91 us
    another operation x10, local copies, waits for them, and re-layouts, tile_weights(): return jnp.tile(flipped, (1, 1, LANES // weight.shape[1]))  1.82 us
  transfers between devices with their start and end apart: 2, of which 1 were waited for; matrix products, arithmetic and copies ran while one was open for 5% of the time, Pallas kernels for 20%

commit v1 on v0

--- a/solution.py
+++ b/solution.py
@@ -21,17 +21,16 @@
 }
 
 
-def tile_weights(weight, chan_in):
-    flipped = jnp.swapaxes(weight, 1, 2)
-    return jnp.tile(flipped, (1, 1, LANES // weight.shape[1]))
-
-
-def build_band(name, tiled_ref, band_ref):
+def build_band(name, weight_ref, band_ref):
     chan, cell_lanes, cells, scale = BANDS[name]
     cell_of_lane = lax.broadcasted_iota(jnp.int32, (chan, LANES), 1) // cell_lanes
     depth = chan * len(cells)
+    chan_out = weight_ref.shape[1]
     for down in range(3):
-        taps = [tiled_ref[3 * down + c].astype(F32) * scale for c in range(3)]
+        taps = []
+        for c in range(3):
+            flipped = (weight_ref[3 * down + c].astype(F32) * scale).T
+            taps.append(jnp.concatenate([flipped] * (LANES // chan_out), axis=1))
         for number, cell in enumerate(cells):
             total = jnp.zeros((chan, LANES), F32)
             if cell is not None:
@@ -123,20 +122,20 @@
     ref[pl.ds((height + 1) * span, span)] = zero
 
 
-def chunks(total, count, body):
+def chunks(total, count, body, first=0):
     steps = total // count
     if steps == 1:
         body(0)
     else:
 
         def step(i, carry):
-            body(i * count)
+            body(lax.rem(i + first, steps) * count)
             return carry
 
         lax.fori_loop(0, steps, step, 0)
 
 
-def unet(height, span, load, emit, bands, scratch):
+def unet(height, span, load, emit, bands, scratch, first=0):
     b_in, b_down2, b_down3, b_up3, b_up2, b_up1, b_out = bands
     win, a1, p1, a2, p2, a3, s2, s1 = scratch
     for ref, rows in ((win, height), (p1, height // 2), (p2, height // 4), (a3, height // 4)):
@@ -204,12 +203,14 @@
         block = lax.broadcasted_iota(jnp.int32, shape, 1)
         emit(g, jnp.sum(jnp.where(lane % 128 // 8 == BLOCKS - 1 - block, spread, 0.0), axis=1))
 
-    chunks(units, count, level1_up)
-
-
-def unit_scratch(height, span):
+    chunks(units, count, level1_up, first)
+
+
+def unit_scratch(height, span, extent):
     def spec(rows, lanes, edge=True):
-        return pltpu.VMEM(((rows + (2 if edge else 0)) * span, BLOCKS, lanes), BF16)
+        pad = 2 if edge else 0
+        flat = extent * rows // height + pad
+        return pltpu.VMEM((max((rows + pad) * span, flat), BLOCKS, lanes), BF16)
 
     return [
         spec(height, 128),
@@ -241,59 +242,156 @@
     build_out(tiled[6], bands[6])
 
 
-def net_kernel(height, span, x_ref, *refs):
-    tiled, out_ref, bands, scratch = refs[:7], refs[7], refs[8:15], refs[15:]
+def peer_id(index, inner):
+    return {"slab": index // inner, "sub": lax.rem(index, inner)}
+
+
+def window_kernel(peers, inner, plane_ref, *refs):
+    tiled, out_ref, bands = refs[:7], refs[7], refs[8:15]
+    scratch = refs[15:23]
+    send, recv, flat, back_send, back, out_sem, in_sem, back_out_sem, back_in_sem = refs[23:]
+    extent = plane_ref.shape[1]
+    cut = extent // peers
+    span = 2 * cut
+    me = lax.axis_index("slab") * inner + lax.axis_index("sub")
+
+    barrier = pltpu.get_barrier_semaphore()
+
+    def greet(k, carry):
+        pl.semaphore_signal(
+            barrier,
+            inc=1,
+            device_id=peer_id(lax.rem(me + k, peers), inner),
+            device_id_type=pl.DeviceIdType.MESH,
+        )
+        return carry
+
+    lax.fori_loop(1, peers, greet, 0)
+    for chan in range(2):
+        plane = plane_ref[chan].astype(F32)
+        send[:, 0, chan] = plane.reshape(peers, cut, extent)
+        send[:, 1, chan] = plane.T.reshape(peers, cut, extent)
+    recv[pl.ds(me, 1)] = send[pl.ds(me, 1)]
+    pl.semaphore_wait(barrier, peers - 1)
+
+    def input_copy(k):
+        peer = lax.rem(me + k, peers)
+        return pltpu.make_async_remote_copy(
+            src_ref=send.at[peer],
+            dst_ref=recv.at[me],
+            send_sem=out_sem.at[k],
+            recv_sem=in_sem.at[k],
+            device_id=peer_id(peer, inner),
+            device_id_type=pl.DeviceIdType.MESH,
+        )
+
+    def result_copy(peer):
+        k = lax.rem(peer + peers - me, peers)
+        return pltpu.make_async_remote_copy(
+            src_ref=back_send.at[peer],
+            dst_ref=back.at[me],
+            send_sem=back_out_sem.at[k],
+            recv_sem=back_in_sem.at[k],
+            device_id=peer_id(peer, inner),
+            device_id_type=pl.DeviceIdType.MESH,
+        )
+
+    def start(k, carry):
+        input_copy(k).start()
+        return carry
+
+    lax.fori_loop(1, peers, start, 0)
     build_all(tiled, bands)
 
-    def load(chan, start, count):
-        return x_ref[chan, pl.ds(pl.multiple_of(start, 16), count), :]
-
-    def emit(start, values):
-        count = values.shape[0]
-        out_ref[pl.ds(pl.multiple_of(start, 16), count), :] = values.astype(out_ref.dtype)
-
-    unet(height, span, load, emit, bands, scratch)
-
-
-def run_net(x, tiled, height, span, dtype):
-    return pl.pallas_call(
-        functools.partial(net_kernel, height, span),
-        out_shape=jax.ShapeDtypeStruct((height * span, 384), dtype),
-        in_specs=[pl.BlockSpec(memory_space=pltpu.VMEM)] * 8,
-        out_specs=pl.BlockSpec(memory_space=pltpu.VMEM),
-        scratch_shapes=BAND_SCRATCH + unit_scratch(height, span),
-        compiler_params=pltpu.CompilerParams(vmem_limit_bytes=48 << 20),
-    )(x, *tiled)
+    def load_flat(chan, begin, count):
+        return plane_ref[chan, pl.ds(pl.multiple_of(begin, 16), count), :]
+
+    def emit_flat(begin, values):
+        flat[pl.ds(pl.multiple_of(begin, 16), values.shape[0]), :] = values
+
+    unet(extent, 1, load_flat, emit_flat, bands, scratch)
+
+    def finish(k, carry):
+        input_copy(k).wait()
+        return carry
+
+    lax.fori_loop(1, peers, finish, 0)
+
+    def load_cross(chan, begin, count):
+        return recv[pl.ds(begin // span, count // span), :, chan].reshape(count, extent)
+
+    def emit_cross(begin, values):
+        rows = values.shape[0] // span
+        values = values.reshape(rows, 2, cut, 3 * extent)
+        pieces = [
+            values[:, run, :, out * extent : (out + 1) * extent]
+            for run in range(2)
+            for out in range(3)
+        ]
+        z = begin // span
+        back_send[pl.ds(z, rows)] = jnp.concatenate(pieces, axis=1).astype(BF16)
+        for row in range(rows):
+
+            @pl.when(z + row != me)
+            def _():
+                result_copy(z + row).start()
+
+            @pl.when(z + row == me)
+            def _():
+                back[pl.ds(me, 1)] = back_send[pl.ds(me, 1)]
+
+    group = max(32, 2 * span) // span
+    unet(peers, span, load_cross, emit_cross, bands, scratch, me // group + 1)
+
+    def settle(k, carry):
+        result_copy(lax.rem(me + k, peers)).wait()
+        return carry
+
+    lax.fori_loop(1, peers, settle, 0)
+
+    def result(run, out):
+        begin = (run * 3 + out) * cut
+        values = back[:, begin : begin + cut, :].astype(F32).reshape(extent, extent)
+        return values.T if run == 1 else values
+
+    out_ref[0] = (result(0, 0) + result(1, 0)) * 0.5
+    out_ref[1] = (flat[:, :extent] + result(1, 1)) * 0.5
+    out_ref[2] = (flat[:, extent : 2 * extent] + result(0, 1)) * 0.5
+    out_ref[3] = (flat[:, 2 * extent :] + result(0, 2) + result(1, 2)) / 3.0
 
 
 def prepare(weights):
     w_in, w_out = weights[0], weights[6]
     tiled_in = jnp.tile(jnp.swapaxes(w_in, 1, 2).reshape(18, 32), (1, 8))
     tiled_out = jnp.tile(jnp.swapaxes(w_out, 0, 1), (8, 1))
-    return [tiled_in] + [tile_weights(w, w.shape[2]) for w in weights[1:6]] + [tiled_out]
+    return [tiled_in] + list(weights[1:6]) + [tiled_out]
 
 
 def shards(image, *weights):
-    tiled = prepare(weights)
     chan, _, extent, _ = image.shape
-    plane = image[:, 0]
     peers = lax.axis_size(AXES)
     cut = extent // peers
-    both = jnp.stack([plane, jnp.swapaxes(plane, 1, 2)])
-    send = jnp.transpose(both.reshape(2, chan, peers, cut, extent), (2, 1, 0, 3, 4))
-    got = lax.all_to_all(send, AXES, split_axis=0, concat_axis=0, tiled=True)
-    cross = jnp.transpose(got, (1, 0, 2, 3, 4)).reshape(chan, peers * 2 * cut, extent)
-    flat = run_net(plane, tiled, extent, 1, F32).reshape(extent, 3, extent)
-    result = run_net(cross, tiled, peers, 2 * cut, BF16).reshape(peers, 2, cut, 3, extent)
-    back = lax.all_to_all(result, AXES, split_axis=0, concat_axis=0, tiled=True)
-    back = jnp.transpose(back, (1, 3, 0, 2, 4)).reshape(2, 3, extent, extent).astype(F32)
-    xz = back[0]
-    yz = jnp.swapaxes(back[1], 1, 2)
-    flow_z = (xz[0] + yz[0]) * 0.5
-    flow_y = (flat[:, 0] + yz[1]) * 0.5
-    flow_x = (flat[:, 1] + xz[1]) * 0.5
-    prob = (flat[:, 2] + xz[2] + yz[2]) / 3.0
-    return jnp.stack([flow_z, flow_y, flow_x, prob])[:, None]
+    sems = [pltpu.SemaphoreType.DMA((peers,))] * 4
+    flows = pl.pallas_call(
+        functools.partial(window_kernel, peers, lax.axis_size("sub")),
+        out_shape=jax.ShapeDtypeStruct((4, extent, extent), F32),
+        in_specs=[pl.BlockSpec(memory_space=pltpu.VMEM)] * 8,
+        out_specs=pl.BlockSpec(memory_space=pltpu.VMEM),
+        scratch_shapes=BAND_SCRATCH
+        + unit_scratch(peers, 2 * cut, extent)
+        + [
+            pltpu.VMEM((peers, 2, chan, cut, extent), F32),
+            pltpu.VMEM((peers, 2, chan, cut, extent), F32),
+            pltpu.VMEM((extent, 3 * extent), F32),
+            pltpu.VMEM((peers, 6 * cut, extent), BF16),
+            pltpu.VMEM((peers, 6 * cut, extent), BF16),
+        ]
+        + sems,
+        compiler_params=pltpu.CompilerParams(
+            vmem_limit_bytes=50 << 20, collective_id=0, has_side_effects=True
+        ),
+    )(image[:, 0], *prepare(weights))
+    return flows[:, None]
 
 
 def solution(mesh):

time: 53.8 us -> 42.2 us (0.78)
  starting transfers between devices: 11.6 us -> 0 us
  Pallas kernels: 30.5 us -> 37.8 us
  local copies, waits for them, and re-layouts: 8.19 us -> 4.16 us
  waiting for transfers between devices: 1.92 us -> 0 us
  other arithmetic: 0.83 us -> 0 us
    all_to_all x2 -> x0, starting transfers between devices: 11.6 us -> none  [the longest x1 7.49 us: shards(): got = lax.all_to_all(send, AXES, split_axis=0, concat_axis=0, tiled=True)]
    pallas_call x2 -> x1, Pallas kernels: 30.5 us -> 37.8 us  [shards(): pl.pallas_call(functools.partial(window_kernel, peers, lax.axis_size('sub...]
    all_to_all x2 -> x0, waiting for transfers between devices: 1.92 us -> none  [the longest x1 1.91 us: shards(): got = lax.all_to_all(send, AXES, split_axis=0, concat_axis=0, tiled=True)]
    transpose x4 -> x0, local copies, waits for them, and re-layouts: 1.83 us -> none  [the longest x1 1.02 us: shards(): both = jnp.stack([plane, jnp.swapaxes(plane, 1, 2)])]
    another operation x10 -> x0, local copies, waits for them, and re-layouts: 1.82 us -> none  [tile_weights(): return jnp.tile(flipped, (1, 1, LANES // weight.shape[1]))]
    broadcast_in_dim x1 -> x0, other arithmetic: 0.73 us -> none  [shards(): return jnp.stack([flow_z, flow_y, flow_x, prob])[:, None]]
  transfers between devices with their start and end apart: 2 -> 0, of which waited for: 1 -> 0; matrix products, arithmetic and copies ran while one was open for 5% -> 0% of each run, Pallas kernels for 20% -> 0%
where the time goes in v1:
time: 42.2 us; the launch traced here: 42 us
  Pallas kernels  37.8 us (90%)
  local copies, waits for them, and re-layouts  4.16 us (10%)
    pallas_call x1, Pallas kernels, shards(): pl.pallas_call(functools.partial(window_kernel, peers, lax.axis_size('sub...  37.8 us
    unnamed x19, local copies, waits for them, and re-layouts  3.92 us

profile of v1, /device:TPU:0, one launch (start us, length us, event | category | flops | bytes accessed | tf_op | source)
XLA Modules:
  0.0 42.0 jit_solution(13484526887372944850)
XLA Ops:
  0.0 0.0 copy-start.6
  0.0 0.7 %copy-done.6 = bf16[9,32,2]{1,2,0:T(2,128)(2,1)S(1)} copy-done((bf16[9,32,2]{1,2,0:T(2,128)(2,1)S(1)}, bf16[9,32,2]{1,2,0:T(2,128)(2,1)}, u32[]{:S(2)}) %copy-start.6) | copy-done | bytes 1176
  0.7 0.0 copy-start.7
  0.7 0.7 %copy-done.7 = bf16[3,32]{1,0:T(4,128)(2,1)S(1)} copy-done((bf16[3,32]{1,0:T(4,128)(2,1)S(1)}, bf16[3,32]{1,0:T(4,128)(2,1)}, u32[]{:S(2)}) %copy-start.7) | copy-done | bytes 216
  1.4 0.1 copy.9
  1.5 0.0 copy-start.5
  1.5 0.1 tile.21.refs_0_
  1.6 0.0 copy-start.4
  1.6 0.7 %copy-done.5 = bf16[9,64,32]{1,2,0:T(8,128)(2,1)S(1)} copy-done((bf16[9,64,32]{1,2,0:T(8,128)(2,1)S(1)}, bf16[9,64,32]{1,2,0:T(8,128)(2,1)}, u32[]{:S(2)}) %copy-start.5) | copy-done | bytes 36888
  2.4 0.1 copy.10.refs_1_
  2.5 0.0 copy-done.4
  2.5 0.0 copy-start
  2.5 0.0 copy-start.1
  2.5 0.0 copy-start.2
  2.5 0.0 copy-start.3
  2.6 0.2 copy.11.refs_2_
  2.8 0.6 %copy-done = bf16[9,64,128]{2,1,0:T(8,128)(2,1)S(1)} copy-done((bf16[9,64,128]{2,1,0:T(8,128)(2,1)S(1)}, bf16[9,64,128]{2,1,0:T(8,128)(2,1)}, u32[]{:S(2)}) %copy-start) | copy-done | bytes 147480
  3.4 0.0 copy-done.1
  3.5 0.0 copy-done.2
  3.5 0.0 copy-done.3
  3.5 37.8 %shard_map.82 = f32[4,128,128]{2,1,0:T(8,128)S(1)} custom-call(bf16[2,128,128]{2,1,0:T(8,128)(2,1)S(1)} %bitcast.9, bf16[18,256]{1,0:T(8,128)(2,1)S(1)} %tile.21.refs_0_, bf16[9,64,32]{2,1,0:T(8,128)(2,1)S(1)} %copy.10.refs_1_, bf16[9,128,64]{2,1,0:T(8,128)(2,1)S(1)} %copy.11.refs_2_, bf16[9,64,128]{2,1,0:T(8,128)(2,1)S(1)} %copy-done, ...), custom_call_target="tpu_custom_call" | custom-call | tf_op jit(solution)/shard_map/pallas_call | solution.py:375
  41.3 0.7 %copy.14 = f32[4,1,128,128]{3,2,1,0:T(8,128)} copy(f32[4,1,128,128]{3,2,1,0:T(8,128)S(1)} %bitcast.7) | data formatting | bytes 524288
  (3 shorter events, 0.0 us)
Async XLA Ops:
  0.0 0.7 %copy-start.6 = (bf16[9,32,2]{1,2,0:T(2,128)(2,1)S(1)}, bf16[9,32,2]{1,2,0:T(2,128)(2,1)}, u32[]{:S(2)}) copy-start(bf16[9,32,2]{1,2,0:T(2,128)(2,1)} %param.9) | copy-start | bytes 3460
  0.7 0.7 %copy-start.7 = (bf16[3,32]{1,0:T(4,128)(2,1)S(1)}, bf16[3,32]{1,0:T(4,128)(2,1)}, u32[]{:S(2)}) copy-start(bf16[3,32]{1,0:T(4,128)(2,1)} %param.15) | copy-start | bytes 580
  1.5 0.9 %copy-start.5 = (bf16[9,64,32]{1,2,0:T(8,128)(2,1)S(1)}, bf16[9,64,32]{1,2,0:T(8,128)(2,1)}, u32[]{:S(2)}) copy-start(bf16[9,64,32]{1,2,0:T(8,128)(2,1)} %param.10) | copy-start | bytes 110596
  1.6 0.9 %copy-start.4 = (bf16[9,128,64]{1,2,0:T(8,128)(2,1)S(1)}, bf16[9,128,64]{1,2,0:T(8,128)(2,1)}, u32[]{:S(2)}) copy-start(bf16[9,128,64]{1,2,0:T(8,128)(2,1)} %param.11) | copy-start | bytes 442372
  2.5 0.9 %copy-start = (bf16[9,64,128]{2,1,0:T(8,128)(2,1)S(1)}, bf16[9,64,128]{2,1,0:T(8,128)(2,1)}, u32[]{:S(2)}) copy-start(bf16[9,64,128]{2,1,0:T(8,128)(2,1)} %refs_3_.1) | copy-start | bytes 442372
  2.5 1.0 %copy-start.1 = (bf16[9,32,64]{2,1,0:T(8,128)(2,1)S(1)}, bf16[9,32,64]{2,1,0:T(8,128)(2,1)}, u32[]{:S(2)}) copy-start(bf16[9,32,64]{2,1,0:T(8,128)(2,1)} %refs_4_.1) | copy-start | bytes 110596
  2.5 1.0 %copy-start.2 = (bf16[9,32,32]{2,1,0:T(8,128)(2,1)S(1)}, bf16[9,32,32]{2,1,0:T(8,128)(2,1)}, u32[]{:S(2)}) copy-start(bf16[9,32,32]{2,1,0:T(8,128)(2,1)} %refs_5_.1) | copy-start | bytes 55300
  2.5 1.0 %copy-start.3 = (bf16[2,1,128,128]{3,2,1,0:T(8,128)(2,1)S(1)}, bf16[2,1,128,128]{3,2,1,0:T(8,128)(2,1)}, u32[]{:S(2)}) copy-start(bf16[2,1,128,128]{3,2,1,0:T(8,128)(2,1)} %param.8) | copy-start | bytes 196612

commit v2 on v1

--- a/solution.py
+++ b/solution.py
@@ -11,6 +11,9 @@
 BLOCKS = 16
 LANES = 256
 AXES = ("slab", "sub")
+UNITS = 32
+LAST_UNITS = 64
+UNROLL = 4
 
 BANDS = {
     "down2": (32, 64, (0, 0, 1, 1, 2, 2, 3, 3, 4, 4, -1, -1), 0.25),
@@ -40,28 +43,32 @@
             band_ref[start : start + chan, :] = total.astype(BF16)
 
 
-def build_in(tiled_ref, band_ref):
+def build_in(weight_ref, band_ref):
     shape = (128, LANES)
     row = lax.broadcasted_iota(jnp.int32, shape, 0)
     cell = lax.broadcasted_iota(jnp.int32, shape, 1) // 32
-    tiled = tiled_ref[...].astype(F32)
     for down in range(3):
         total = jnp.zeros(shape, F32)
-        for chan in range(2):
-            for c in range(3):
-                index = (3 * down + c) * 2 + chan
-                total = jnp.where(row - 16 * chan - cell == c, tiled[index : index + 1, :], total)
+        for c in range(3):
+            flipped = weight_ref[3 * down + c].astype(F32).T
+            tiled = jnp.concatenate([flipped] * 8, axis=1)
+            for chan in range(2):
+                here = row - 16 * chan - cell == c
+                total = jnp.where(here, tiled[chan : chan + 1, :], total)
         band_ref[128 * down : 128 * down + 128, :] = total.astype(BF16)
 
 
-def build_out(tiled_ref, band_ref):
+def build_out(weight_ref, band_ref):
     shape = (LANES, 128)
-    keep = lax.broadcasted_iota(jnp.int32, shape, 0) // 32 == lax.broadcasted_iota(
-        jnp.int32, shape, 1
-    ) % 8
+    lane = lax.broadcasted_iota(jnp.int32, shape, 1)
+    keep = lax.broadcasted_iota(jnp.int32, shape, 0) // 32 == lane % 8
+    total = jnp.zeros(shape, F32)
+    flipped = weight_ref[...].astype(F32).T
+    tiled = jnp.concatenate([flipped] * 8, axis=0)
     for out in range(3):
-        value = tiled_ref[:, out : out + 1].astype(F32)
-        band_ref[:, 128 * out : 128 * out + 128] = jnp.where(keep, value, 0.0).astype(BF16)
+        value = tiled[:, out : out + 1]
+        total = jnp.where(keep & (lane // 32 == out), value, total)
+    band_ref[...] = total.astype(BF16)
 
 
 def neighbours(values):
@@ -122,30 +129,33 @@
     ref[pl.ds((height + 1) * span, span)] = zero
 
 
+def chunk_units(total, span, most):
+    return min(max(most, 2 * span), total)
+
+
 def chunks(total, count, body, first=0):
     steps = total // count
     if steps == 1:
-        body(0)
+        body(0, count)
     else:
 
         def step(i, carry):
-            body(lax.rem(i + first, steps) * count)
+            body(lax.rem(i + first, steps) * count, count)
             return carry
 
-        lax.fori_loop(0, steps, step, 0)
+        lax.fori_loop(0, steps, step, 0, unroll=min(steps, UNROLL))
 
 
 def unet(height, span, load, emit, bands, scratch, first=0):
     b_in, b_down2, b_down3, b_up3, b_up2, b_up1, b_out = bands
-    win, a1, p1, a2, p2, a3, s2, s1 = scratch
+    win, a1, p1, a2, p2, a3, s2, s1, spread = scratch
     for ref, rows in ((win, height), (p1, height // 2), (p2, height // 4), (a3, height // 4)):
         clear_edges(ref, rows, span)
     clear_edges(s2, height // 2, span)
     clear_edges(s1, height, span)
     units = height * span
-    count = max(32, 2 * span)
-
-    def fill(g):
+
+    def fill(g, count):
         shape = (count, BLOCKS, 128)
         lane = lax.broadcasted_iota(jnp.int32, shape, 2)
         block = lax.broadcasted_iota(jnp.int32, shape, 1)
@@ -158,52 +168,66 @@
         merged = jnp.where(lane < 16, rolled[0], rolled[1])
         win[pl.ds(g + span, count)] = jnp.where(outside, 0.0, merged).astype(BF16)
 
-    chunks(units, count, fill)
-
-    def level1(g):
+    chunks(units, chunk_units(units, span, 32), fill)
+
+    def level1(g, count):
         values = conv(win, b_in, g, count, span)
         a1[pl.ds(g, count)] = values.astype(BF16)
         store_narrow(p1, g // 2 + span, pair_sum(values, span))
 
-    chunks(units, count, level1)
-
-    def level2(g):
+    chunks(units, chunk_units(units, span, UNITS), level1)
+
+    def level2(g, count):
         values = conv(p1, b_down2, g, count, span)
         a2[pl.ds(g, count)] = values.astype(BF16)
         store_wide(p2, g // 2 + span, pair_sum(values, span))
 
-    chunks(units // 2, count, level2)
-
-    def level3(g):
+    chunks(units // 2, chunk_units(units // 2, span, UNITS), level2)
+
+    def level3(g, count):
         store_wide(a3, g + span, conv(p2, b_down3, g, count, span))
 
-    chunks(units // 4, count, level3)
-
-    def level3_up(g):
+    chunks(units // 4, chunk_units(units // 4, span, UNITS), level3)
+
+    def level3_up(g, count):
         values = twice(conv(a3, b_up3, g, count, span), span)
         skip = a2[pl.ds(2 * g, 2 * count)].astype(F32)
         store_narrow(s2, 2 * g + span, values + skip)
 
-    chunks(units // 4, count, level3_up)
-
-    def level2_up(g):
+    chunks(units // 4, chunk_units(units // 4, span, UNITS), level3_up)
+
+    def level2_up(g, count):
         values = twice(conv(s2, b_up2, g, count, span), span)
         skip = a1[pl.ds(2 * g, 2 * count)].astype(F32)
         store_narrow(s1, 2 * g + span, values + skip)
 
-    chunks(units // 2, count, level2_up)
-
-    def level1_up(g):
+    chunks(units // 2, chunk_units(units // 2, span, UNITS), level2_up)
+
+    def level1_up(g, count):
         values = conv(s1, b_up1, g, count, span).astype(BF16)
-        spread = jnp.dot(
+        spread[pl.ds(0, count * BLOCKS), :] = jnp.dot(
             values.reshape(count * BLOCKS, LANES), b_out[...], preferred_element_type=F32
-        ).reshape(count, BLOCKS, 384)
-        shape = (count, BLOCKS, 384)
-        lane = lax.broadcasted_iota(jnp.int32, shape, 2)
-        block = lax.broadcasted_iota(jnp.int32, shape, 1)
-        emit(g, jnp.sum(jnp.where(lane % 128 // 8 == BLOCKS - 1 - block, spread, 0.0), axis=1))
-
-    chunks(units, count, level1_up, first)
+        )
+        lane = lax.broadcasted_iota(jnp.int32, (count, 128), 1)
+        quads = []
+        for quad in range(4):
+            total = None
+            for part in range(4):
+                row = BLOCKS - 1 - (4 * quad + part)
+                piece = spread[pl.ds(row, count, stride=BLOCKS), :]
+                total = piece if part == 0 else jnp.where(lane % 32 // 8 == part, piece, total)
+            quads.append(total)
+        outs = []
+        for out in range(3):
+            total = None
+            for quad in range(4):
+                shift = 32 * (quad - out) % 128
+                piece = quads[quad] if shift == 0 else pltpu.roll(quads[quad], shift, 1)
+                total = piece if quad == 0 else jnp.where(lane // 32 == quad, piece, total)
+            outs.append(total)
+        emit(g, jnp.concatenate(outs, axis=1))
+
+    chunks(units, chunk_units(units, span, LAST_UNITS), level1_up, first)
 
 
 def unit_scratch(height, span, extent):
@@ -221,6 +245,7 @@
         spec(height // 4, 512),
         spec(height // 2, 384),
         spec(height, 384),
+        pltpu.VMEM((max(LAST_UNITS, 2 * span) * BLOCKS, 128), F32),
     ]
 
 
@@ -231,7 +256,7 @@
     pltpu.VMEM((1536, 256), BF16),
     pltpu.VMEM((1152, 256), BF16),
     pltpu.VMEM((1152, 256), BF16),
-    pltpu.VMEM((256, 384), BF16),
+    pltpu.VMEM((256, 128), BF16),
 ]
 
 
@@ -246,10 +271,18 @@
     return {"slab": index // inner, "sub": lax.rem(index, inner)}
 
 
-def window_kernel(peers, inner, plane_ref, *refs):
-    tiled, out_ref, bands = refs[:7], refs[7], refs[8:15]
-    scratch = refs[15:23]
-    send, recv, flat, back_send, back, out_sem, in_sem, back_out_sem, back_in_sem = refs[23:]
+def window_kernel(peers, inner, image_ref, *refs):
+    given, out_ref, bands = refs[:7], refs[7], refs[8:15]
+    scratch = refs[15:24]
+    send, recv, flat, back_send, back, out_sem, in_sem, back_out_sem, back_in_sem = refs[24:33]
+    plane_ref, weights, local_sem = refs[33], refs[34:41], refs[41]
+    copies = [pltpu.make_async_copy(image_ref.at[:, 0], plane_ref, local_sem.at[0])]
+    for number in range(7):
+        copies.append(
+            pltpu.make_async_copy(given[number], weights[number], local_sem.at[1 + number])
+        )
+    for copy in copies:
+        copy.start()
     extent = plane_ref.shape[1]
     cut = extent // peers
     span = 2 * cut
@@ -267,6 +300,7 @@
         return carry
 
     lax.fori_loop(1, peers, greet, 0)
+    copies[0].wait()
     for chan in range(2):
         plane = plane_ref[chan].astype(F32)
         send[:, 0, chan] = plane.reshape(peers, cut, extent)
@@ -301,7 +335,9 @@
         return carry
 
     lax.fori_loop(1, peers, start, 0)
-    build_all(tiled, bands)
+    for copy in copies[1:]:
+        copy.wait()
+    build_all(weights, bands)
 
     def load_flat(chan, begin, count):
         return plane_ref[chan, pl.ds(pl.multiple_of(begin, 16), count), :]
@@ -340,7 +376,7 @@
             def _():
                 back[pl.ds(me, 1)] = back_send[pl.ds(me, 1)]
 
-    group = max(32, 2 * span) // span
+    group = chunk_units(peers * span, span, LAST_UNITS) // span
     unet(peers, span, load_cross, emit_cross, bands, scratch, me // group + 1)
 
     def settle(k, carry):
@@ -358,13 +394,6 @@
     out_ref[1] = (flat[:, :extent] + result(1, 1)) * 0.5
     out_ref[2] = (flat[:, extent : 2 * extent] + result(0, 1)) * 0.5
     out_ref[3] = (flat[:, 2 * extent :] + result(0, 2) + result(1, 2)) / 3.0
-
-
-def prepare(weights):
-    w_in, w_out = weights[0], weights[6]
-    tiled_in = jnp.tile(jnp.swapaxes(w_in, 1, 2).reshape(18, 32), (1, 8))
-    tiled_out = jnp.tile(jnp.swapaxes(w_out, 0, 1), (8, 1))
-    return [tiled_in] + list(weights[1:6]) + [tiled_out]
 
 
 def shards(image, *weights):
@@ -375,7 +404,7 @@
     flows = pl.pallas_call(
         functools.partial(window_kernel, peers, lax.axis_size("sub")),
         out_shape=jax.ShapeDtypeStruct((4, extent, extent), F32),
-        in_specs=[pl.BlockSpec(memory_space=pltpu.VMEM)] * 8,
+        in_specs=[pl.BlockSpec(memory_space=pl.ANY)] * 8,
         out_specs=pl.BlockSpec(memory_space=pltpu.VMEM),
         scratch_shapes=BAND_SCRATCH
         + unit_scratch(peers, 2 * cut, extent)
@@ -386,11 +415,14 @@
             pltpu.VMEM((peers, 6 * cut, extent), BF16),
             pltpu.VMEM((peers, 6 * cut, extent), BF16),
         ]
-        + sems,
+        + sems
+        + [pltpu.VMEM((chan, extent, extent), BF16)]
+        + [pltpu.VMEM(weight.shape, BF16) for weight in weights]
+        + [pltpu.SemaphoreType.DMA((8,))],
         compiler_params=pltpu.CompilerParams(
             vmem_limit_bytes=50 << 20, collective_id=0, has_side_effects=True
         ),
-    )(image[:, 0], *prepare(weights))
+    )(image, *weights)
     return flows[:, None]
 
 

time: 42.2 us -> 37.5 us (0.89)
  Pallas kernels: 37.8 us -> 33.7 us
  local copies, waits for them, and re-layouts: 4.16 us -> 3.56 us
    pallas_call x1, Pallas kernels: 37.8 us -> 33.7 us  [shards(): pl.pallas_call(functools.partial(window_kernel, peers, lax.axis_size('sub...]
    unnamed x19 -> x16, local copies, waits for them, and re-layouts: 3.92 us -> 3.56 us
where the time goes in v2:
time: 37.5 us; the launch traced here: 37.3 us
  Pallas kernels  33.7 us (90%)
  local copies, waits for them, and re-layouts  3.56 us (9%)
    pallas_call x1, Pallas kernels, shards(): pl.pallas_call(functools.partial(window_kernel, peers, lax.axis_size('sub...  33.7 us
    unnamed x16, local copies, waits for them, and re-layouts  3.56 us

profile of v2, /device:TPU:0, one launch (start us, length us, event | category | flops | bytes accessed | tf_op | source)
XLA Modules:
  0.0 37.3 jit_solution(17744719254472047652)
XLA Ops:
  0.0 0.0 copy-start.5
  0.0 0.9 %copy.9.refs_0_ = bf16[9,32,2]{2,1,0:T(8,128)(2,1)S(1)} copy(bf16[9,32,2]{1,2,0:T(2,128)(2,1)} %param.9) | data formatting | bytes 2304 | tf_op args[1]
  0.9 1.0 %copy.10.refs_1_ = bf16[9,64,32]{2,1,0:T(8,128)(2,1)S(1)} copy(bf16[9,64,32]{1,2,0:T(8,128)(2,1)} %param.10) | data formatting | bytes 73728 | tf_op args[2]
  1.9 0.0 copy-done.5
  1.9 0.0 copy-start
  1.9 0.0 copy-start.1
  1.9 0.0 copy-start.2
  1.9 0.0 copy-start.3
  1.9 0.0 copy-start.4
  2.0 0.2 copy.11.refs_2_
  2.2 0.6 %copy-done = bf16[9,64,128]{2,1,0:T(8,128)(2,1)S(1)} copy-done((bf16[9,64,128]{2,1,0:T(8,128)(2,1)S(1)}, bf16[9,64,128]{2,1,0:T(8,128)(2,1)}, u32[]{:S(2)}) %copy-start) | copy-done | bytes 147480
  2.8 0.0 copy-done.1
  2.9 0.0 copy-done.2
  2.9 0.0 copy-done.3
  2.9 0.0 copy-done.4
  2.9 33.7 %shard_map.82 = f32[4,128,128]{2,1,0:T(8,128)S(1)} custom-call(bf16[2,1,128,128]{3,2,1,0:T(8,128)(2,1)S(1)} %copy-done.3, bf16[9,32,2]{2,1,0:T(8,128)(2,1)S(1)} %copy.9.refs_0_, bf16[9,64,32]{2,1,0:T(8,128)(2,1)S(1)} %copy.10.refs_1_, bf16[9,128,64]{2,1,0:T(8,128)(2,1)S(1)} %copy.11.refs_2_, bf16[9,64,128]{2,1,0:T(8,128)(2,1)S(1)} %copy-done, ...), custom_call_target="tpu_custom_call" | custom-call | tf_op jit(solution)/shard_map/pallas_call | solution.py:404
  36.6 0.7 %copy.14 = f32[4,1,128,128]{3,2,1,0:T(8,128)} copy(f32[4,1,128,128]{3,2,1,0:T(8,128)S(1)} %bitcast.3) | data formatting | bytes 524288
Async XLA Ops:
  0.0 1.9 %copy-start.5 = (bf16[9,128,64]{1,2,0:T(8,128)(2,1)S(1)}, bf16[9,128,64]{1,2,0:T(8,128)(2,1)}, u32[]{:S(2)}) copy-start(bf16[9,128,64]{1,2,0:T(8,128)(2,1)} %param.11) | copy-start | bytes 442372
  1.9 0.9 %copy-start = (bf16[9,64,128]{2,1,0:T(8,128)(2,1)S(1)}, bf16[9,64,128]{2,1,0:T(8,128)(2,1)}, u32[]{:S(2)}) copy-start(bf16[9,64,128]{2,1,0:T(8,128)(2,1)} %refs_3_.1) | copy-start | bytes 442372
  1.9 1.0 %copy-start.1 = (bf16[9,32,64]{2,1,0:T(8,128)(2,1)S(1)}, bf16[9,32,64]{2,1,0:T(8,128)(2,1)}, u32[]{:S(2)}) copy-start(bf16[9,32,64]{2,1,0:T(8,128)(2,1)} %refs_4_.1) | copy-start | bytes 110596
  1.9 1.0 %copy-start.2 = (bf16[9,32,32]{2,1,0:T(8,128)(2,1)S(1)}, bf16[9,32,32]{2,1,0:T(8,128)(2,1)}, u32[]{:S(2)}) copy-start(bf16[9,32,32]{2,1,0:T(8,128)(2,1)} %refs_5_.1) | copy-start | bytes 55300
  1.9 1.0 %copy-start.3 = (bf16[2,1,128,128]{3,2,1,0:T(8,128)(2,1)S(1)}, bf16[2,1,128,128]{3,2,1,0:T(8,128)(2,1)}, u32[]{:S(2)}) copy-start(bf16[2,1,128,128]{3,2,1,0:T(8,128)(2,1)} %image_ref.1) | copy-start | bytes 196612
  1.9 1.0 %copy-start.4 = (bf16[3,32]{1,0:T(4,128)(2,1)S(1)}, bf16[3,32]{1,0:T(4,128)(2,1)}, u32[]{:S(2)}) copy-start(bf16[3,32]{1,0:T(4,128)(2,1)} %refs_6_.1) | copy-start | bytes 580
